TPU v7x, 256 devices: a whole 4x4x8 slice. The times are simulated.
256 devices in a mesh: lon: 16 (over z, x_hi), lat: 16 (over y, x_lo, core).
Axes of the slice: x: 4 (x_hi: 2, x_lo: 2; x = x_hi * 2 + x_lo), y: 4, z: 8, core: 2. Of those that a mesh axis runs over, the one named last changes fastest.
Arguments:
- tracers: float32 [2, 8, 2048, 4096], P(None, None, 'lat', 'lon'), may hold values from -6 to 6
- zonal_vel: float32 [8, 2048, 4096], P(None, 'lat', 'lon'), may hold values from -3 to 3
- merid_vel: float32 [8, 2048, 4096], P(None, 'lat', 'lon'), may hold values from -3 to 3
- thickness: float32 [8, 2048, 4096], P(None, 'lat', 'lon'), may hold values from 0.5 to 2
- land_sea: int32 [8, 2048, 4096], P(None, 'lat', 'lon'), may hold values from 0 to 1, as said below
- cell_dx: float32 [2048, 4096], P('lat', 'lon'), may hold values from 0.5 to 1.5
- cell_dy: float32 [2048, 4096], P('lat', 'lon'), may hold values from 0.5 to 1.5
- fold_partner: int32 [4096], P('lon'), may hold values from 0 to 4095, as said below
Outputs:
- new_tracers: float32 [2, 8, 2048, 4096], P(None, None, 'lat', 'lon')
Inputs may be any that keep to these rules, and one draw needn't show every extreme that they name: In each column the ocean cells are the top levels: land_sea is 1 on levels above a column depth of 1 to 8 levels and 0 below it. fold_partner[i] = (4095 - i + p) mod 4096 with one pivot p of 1 to 255 for all i.
All inputs are finite; a program needn't handle non-finite values.
Results may differ from a plain program's by a relative error of at most 0.00002.
Values sent between devices are 32-bit elements; how exact they have to be, the bound alone decides.
No kernel may reach another device: no remote copies, remote signals or barrier semaphores. Data moves between devices by JAX's collectives and lax.ppermute only.
A program may use at most 128 MiB of HBM per device.

v0:
```python
import jax
import jax.numpy as jnp
from jax import lax
from jax.sharding import PartitionSpec as P

TIME_STEP = 0.2
DIFFUSIVITY = 0.25


def extended(array, sides, width, wrap):
    for axis, dim in sides:
        count, length = (lax.axis_size(axis), array.shape[dim])
        up = [(i, (i + 1) % count) for i in range(count if wrap else count - 1)]
        down = [(j, i) for i, j in up]
        last = lax.slice_in_dim(array, length - width, length, axis=dim)
        leading = lax.slice_in_dim(array, 0, width, axis=dim)
        before = lax.ppermute(last, axis, up)
        after = lax.ppermute(leading, axis, down)
        array = jnp.concatenate([before, array, after], axis=dim)
    return array


def from_behind(array, axis, by):
    count = lax.axis_size(axis)
    return lax.ppermute(array, axis, [(i, (i + by) % count) for i in range(count)])


def shifted(value, axis, steps):
    count = lax.axis_size(axis)
    leading, last = (max(0, -steps), min(count, count - steps))
    return lax.ppermute(value, axis, [(source, source + steps) for source in range(leading, last)])


def tendency(
    trac_lon,
    trac_lat,
    thick_lon,
    thick_lat,
    dx_lon,
    dx_lat,
    dy_lon,
    dy_lat,
    u_faces,
    v_faces,
    volume,
):
    dy_u = 0.5 * (dy_lon[:, :-1] + dy_lon[:, 1:])
    dx_u = 0.5 * (dx_lon[:, :-1] + dx_lon[:, 1:])
    thick_u = jnp.minimum(thick_lon[..., :-1], thick_lon[..., 1:])
    trans_u = u_faces * dy_u * thick_u
    diff_u = DIFFUSIVITY * dy_u * thick_u / dx_u
    flux_x = trans_u * 0.5 * (trac_lon[..., :-1] + trac_lon[..., 1:]) - diff_u * (
        trac_lon[..., 1:] - trac_lon[..., :-1]
    )
    dx_v = 0.5 * (dx_lat[:-1, :] + dx_lat[1:, :])
    dy_v = 0.5 * (dy_lat[:-1, :] + dy_lat[1:, :])
    thick_v = jnp.minimum(thick_lat[..., :-1, :], thick_lat[..., 1:, :])
    trans_v = v_faces * dx_v * thick_v
    diff_v = DIFFUSIVITY * dx_v * thick_v / dy_v
    flux_y = trans_v * 0.5 * (trac_lat[..., :-1, :] + trac_lat[..., 1:, :]) - diff_v * (
        trac_lat[..., 1:, :] - trac_lat[..., :-1, :]
    )
    divergence = flux_x[..., 1:] - flux_x[..., :-1] + (flux_y[..., 1:, :] - flux_y[..., :-1, :])
    return -divergence / volume


def partner_window(top_rows, fold_partner):
    cycle_size = lax.axis_size("lon")
    cols_here = top_rows.shape[2]
    total = cycle_size * cols_here
    wanted = jnp.concatenate(
        [(fold_partner[:1] + 1) % total, fold_partner, (fold_partner[-1:] - 1 + total) % total]
    )
    gathered = lax.all_gather(top_rows, "lon", axis=2, tiled=True)
    return jnp.take(gathered, wanted, axis=2)


def extend(stack, fold_partner):
    lon_side = extended(stack, (("lon", 2),), 1, True)
    lat_side = extended(stack, (("lat", 1),), 1, False)
    ghost_row = partner_window(stack[:, -1:, :], fold_partner)[:, 0, 1:-1]
    at_top = lax.axis_index("lat") == lax.axis_size("lat") - 1
    upper_row = jnp.where(at_top, ghost_row, lat_side[:, -1, :])
    lat_side = jnp.concatenate([lat_side[:, :-1, :], upper_row[:, None, :]], axis=1)
    return (lon_side, lat_side)


def section_by_section(
    tracers, zonal_vel, merid_vel, thickness, sea_mask, wet_thick, cell_dx, cell_dy, fold_partner
):
    levels = thickness.shape[0]
    rows_here = thickness.shape[1]
    cols_here = thickness.shape[2]
    volume = cell_dx * cell_dy * thickness
    geometry = jnp.concatenate([wet_thick, cell_dx[None], cell_dy[None]], axis=0)
    flat_tracers = tracers.reshape(2 * levels, rows_here, cols_here)
    west_u = from_behind(zonal_vel[:, :, -1:], "lon", 1)
    u_faces = jnp.concatenate([west_u, zonal_vel], axis=2)
    south_v = shifted(merid_vel[:, -1:, :], "lat", 1)
    v_faces = jnp.concatenate([south_v, merid_vel], axis=1)
    geo_lon, geo_lat = extend(geometry, fold_partner)
    trac_lon, trac_lat = extend(flat_tracers, fold_partner)

    def operator(field_lon, field_lat):
        return tendency(
            field_lon.reshape(2, levels, rows_here, cols_here + 2),
            field_lat.reshape(2, levels, rows_here + 2, cols_here),
            geo_lon[:levels],
            geo_lat[:levels],
            geo_lon[levels],
            geo_lat[levels],
            geo_lon[levels + 1],
            geo_lat[levels + 1],
            u_faces,
            v_faces,
            volume,
        )

    first = operator(trac_lon, trac_lat)
    section = tracers + TIME_STEP * first
    section_lon, section_lat = extend(
        section.reshape(2 * levels, rows_here, cols_here), fold_partner
    )
    second = operator(section_lon, section_lat)
    return sea_mask * (tracers + 0.5 * TIME_STEP * (first + second))


def shards(tracers, zonal_vel, merid_vel, thickness, land_sea, cell_dx, cell_dy, fold_partner):
    sea_mask = land_sea.astype(jnp.float32)
    wet_thick = thickness * sea_mask
    return section_by_section(
        tracers,
        zonal_vel,
        merid_vel,
        thickness,
        sea_mask,
        wet_thick,
        cell_dx,
        cell_dy,
        fold_partner,
    )


def solution(mesh):
    return jax.shard_map(
        shards,
        mesh=mesh,
        in_specs=(
            P(None, None, "lat", "lon"),
            P(None, "lat", "lon"),
            P(None, "lat", "lon"),
            P(None, "lat", "lon"),
            P(None, "lat", "lon"),
            P("lat", "lon"),
            P("lat", "lon"),
            P("lon"),
        ),
        out_specs=P(None, None, "lat", "lon"),
        check_vma=False,
    )
```

profile of v0, /device:TPU:116, one launch (start us, length us, event | category | flops | bytes accessed | tf_op | source)
XLA Modules:
  0.0 362.2 jit_solution(13244162745184583832)
XLA Ops:
  0.0 1.0 mul.221
  1.0 2.8 convert_multiply_fusion
  3.8 1.2 pad_maximum_fusion.8
  5.0 3.0 copy.218
  8.0 1.4 fusion.28
  9.4 3.1 collective-permute-start.1
  13.0 2.5 copy.216
  15.5 1.3 slice.243
  16.8 5.2 %collective-permute-start = (f32[8,128,1]{1,0,2:T(8,128)}, f32[8,128,1]{1,0,2:T(8,128)}, u32[]{:S(2)}, u32[]{:S(2)}) collective-permute-start(f32[8,128,1]{1,0,2:T(8,128)} %slice.243), channel_id=1, source_target_pairs={{0,16},{16,32},{32,48},{48,64},{64,80},{80,96},{96,112},{112,128},... | collective-permute-start | bytes 12296 | tf_op jit(solution)/shard_map/ppermute | solution.py:25
  22.0 1.5 fusion.29
  23.5 0.8 copy.251
  24.3 1.9 collective-permute-start.6
  26.8 0.8 copy.253
  27.6 4.1 %collective-permute-start.8 = (f32[16,1,256]{0,2,1:T(8,128)S(1)}, f32[16,1,256]{0,2,1:T(8,128)}, u32[]{:S(2)}, u32[]{:S(2)}) collective-permute-start(f32[16,1,256]{0,2,1:T(8,128)S(1)} %copy.253), channel_id=1, source_target_pairs={{0,1},{1,2},{2,3},{3,4},{4,5},{5,6},{6,7},{7,8},{8,9},{9,10},{10,1... | collective-permute-start | bytes 49160 | tf_op jit(solution)/shard_map/ppermute | solution.py:17
  31.8 1.6 fusion.26
  35.2 70.0 %all_gather.10 = f32[16,1,4096]{0,2,1:T(8,128)} all-gather(f32[16,1,256]{0,2,1:T(8,128)S(1)} %copy.253), channel_id=1, replica_groups=mesh['lon'=16,'lat'=16] {'lon'}, dimensions={2}, use_global_device_ids=true | all-gather | bytes 278528 | tf_op jit(solution)/shard_map/all_gather | solution.py:74
  105.2 1.6 constant_dynamic-update-slice_fusion
  108.7 72.2 %all_gather.9 = f32[10,1,4096]{0,2,1:T(8,128)} all-gather(f32[10,1,256]{0,2,1:T(8,128)} %copy.251), channel_id=1, replica_groups=mesh['lon'=16,'lat'=16] {'lon'}, dimensions={2}, use_global_device_ids=true | all-gather | bytes 174080 | tf_op jit(solution)/shard_map/all_gather | solution.py:74
  180.9 2.9 copy.222
  183.8 2.3 convert_element_type.3
  186.0 2.1 copy.226
  188.2 2.1 copy.228
  190.3 1.3 slice.255
  191.6 1.5 copy.252
  193.0 1.4 slice.211
  195.2 3.3 gather_fusion
  198.5 3.3 gather_fusion.1
  201.9 3.5 collective-permute-start.4
  205.4 1.0 maximum_bitcast_fusion
  207.8 1.9 collective-permute-start.7
  209.8 2.9 fusion.14
  212.7 2.9 copy.225
  215.6 2.9 copy.230
  218.5 2.4 collective-permute-start.5
  220.9 1.3 copy.227
  222.2 4.2 %collective-permute-start.9 = (f32[16,1,256]{0,2,1:T(8,128)}, f32[16,1,256]{0,2,1:T(8,128)}, u32[]{:S(2)}, u32[]{:S(2)}) collective-permute-start(f32[16,1,256]{0,2,1:T(8,128)} %copy.254), channel_id=1, source_target_pairs={{1,0},{2,1},{3,2},{4,3},{5,4},{6,5},{7,6},{8,7},{9,8},{10,9},{11,1... | collective-permute-start | bytes 49160 | tf_op jit(solution)/shard_map/ppermute | solution.py:18
  226.5 1.3 copy.229
  227.8 5.1 %multiply_subtract_fusion.1 = f32[2,8,128,257]{3,2,1,0:T(8,128)} fusion(f32[2,8,128,1]{3,2,1,0:T(8,128)} %copy.229, f32[2,8,128,256]{3,2,1,0:T(8,128)S(1)} %copy-done, f32[2,8,128,1]{3,2,1,0:T(8,128)} %copy.227, f32[8,128,257]{2,1,0:T(8,128)} %copy.230, f32[8,128,257]{2,1,0:T(8,128)} %copy.225), kind=kLoop, calls=%fused_computation.8 | loop fusion | flops 3684352 | bytes 6324224 | tf_op jit(solution)/shard_map/sub | solution.py:52
  233.0 1.7 fusion.21
  234.6 1.0 copy.234
  235.6 1.6 copy.232
  238.0 1.0 maximum_maximum_fusion
  239.2 2.4 fusion.11
  241.6 1.0 fusion.20
  242.8 1.0 copy.236
  243.8 1.6 dynamic-update-slice.1
  245.4 2.9 multiply_subtract_fusion.3
  248.9 2.2 multiply_add_fusion
  251.1 1.9 fusion.24
  253.2 1.6 copy.241
  254.7 2.2 collective-permute-start.10
  257.0 2.1 copy.243
  259.1 1.3 collective-permute-start.11
  260.5 71.2 %all_gather.11 = f32[16,1,4096]{0,2,1:T(8,128)} all-gather(f32[16,1,256]{0,2,1:T(8,128)S(1)} %copy.255), channel_id=1, replica_groups=mesh['lon'=16,'lat'=16] {'lon'}, dimensions={2}, use_global_device_ids=true | all-gather | bytes 278528 | tf_op jit(solution)/shard_map/all_gather | solution.py:74
  331.8 1.9 collective-permute-start.12
  333.7 2.6 gather_fusion.2
  337.1 4.5 %collective-permute-start.13 = (f32[16,1,256]{0,2,1:T(8,128)}, f32[16,1,256]{0,2,1:T(8,128)S(1)}, u32[]{:S(2)}, u32[]{:S(2)}) collective-permute-start(f32[16,1,256]{0,2,1:T(8,128)} %copy.256), channel_id=1, source_target_pairs={{1,0},{2,1},{3,2},{4,3},{5,4},{6,5},{7,6},{8,7},{9,8},{10,9},{11,1... | collective-permute-start | bytes 49160 | tf_op jit(solution)/shard_map/ppermute | solution.py:18
  341.6 2.1 copy.242
  343.8 2.0 copy.244
  345.8 6.3 %multiply_subtract_fusion = f32[2,8,128,257]{3,2,1,0:T(8,128)} fusion(f32[2,8,128,1]{3,2,1,0:T(8,128)} %copy.244, f32[2,8,128,256]{3,2,1,0:T(8,128)} %copy-done.1, f32[2,8,128,1]{3,2,1,0:T(8,128)} %copy.242, f32[8,128,257]{2,1,0:T(8,128)} %copy.230, f32[8,128,257]{2,1,0:T(8,128)} %copy.225), kind=kLoop, calls=%fused_computation.7 | loop fusion | flops 3684352 | bytes 6324224 | tf_op jit(solution)/shard_map/sub | solution.py:52
  352.8 1.0 fusion.19
  353.9 1.0 copy.246
  354.9 3.5 multiply_subtract_fusion.2
  359.6 2.6 fusion.9
  (71 shorter events, 10.3 us)
Async XLA Ops:
  1.0 2.8 copy-start.8
  1.0 2.8 copy-start.9
  5.0 21.2 %copy-start = (f32[2,8,128,256]{3,2,1,0:T(8,128)S(1)}, f32[2,8,128,256]{3,2,1,0:T(8,128)}, u32[]{:S(2)}) copy-start(f32[2,8,128,256]{3,2,1,0:T(8,128)} %param.10) | copy-start | bytes 6291460
  9.4 192.4 %collective-permute-start.1 = (f32[10,128,1]{1,2,0:T(1,128)}, f32[10,128,1]{1,2,0:T(1,128)}, u32[]{:S(2)}, u32[]{:S(2)}) collective-permute-start(f32[10,128,1]{1,2,0:T(1,128)} %get-tuple-element.27), channel_id=1, source_target_pairs={{0,16},{16,32},{32,48},{48,64},{64,80},{80,96},{96,112},{112,128},... | collective-permute-start | bytes 15368 | tf_op jit(solution)/shard_map/ppermute | solution.py:17
  12.5 189.4 %collective-permute-start.2 = (f32[10,128,1]{1,2,0:T(1,128)}, f32[10,128,1]{1,2,0:T(1,128)}, u32[]{:S(2)}, u32[]{:S(2)}) collective-permute-start(f32[10,128,1]{1,2,0:T(1,128)} %get-tuple-element.28), channel_id=1, source_target_pairs={{16,0},{32,16},{48,32},{64,48},{80,64},{96,80},{112,96},{128,112},... | collective-permute-start | bytes 15368 | tf_op jit(solution)/shard_map/ppermute | solution.py:18
  16.8 191.1 %collective-permute-start = (f32[8,128,1]{1,0,2:T(8,128)}, f32[8,128,1]{1,0,2:T(8,128)}, u32[]{:S(2)}, u32[]{:S(2)}) collective-permute-start(f32[8,128,1]{1,0,2:T(8,128)} %slice.243), channel_id=1, source_target_pairs={{0,16},{16,32},{32,48},{48,64},{64,80},{80,96},{96,112},{112,128},... | collective-permute-start | bytes 12296 | tf_op jit(solution)/shard_map/ppermute | solution.py:25
  24.3 211.3 %collective-permute-start.6 = (f32[10,1,256]{0,2,1:T(8,128)}, f32[10,1,256]{0,2,1:T(8,128)}, u32[]{:S(2)}, u32[]{:S(2)}) collective-permute-start(f32[10,1,256]{0,2,1:T(8,128)} %copy.251), channel_id=1, source_target_pairs={{0,1},{1,2},{2,3},{3,4},{4,5},{5,6},{6,7},{7,8},{8,9},{9,10},{10,1... | collective-permute-start | bytes 30728 | tf_op jit(solution)/shard_map/ppermute | solution.py:17
  27.6 5.8 %copy-start.15 = (s32[256]{0:T(256)S(1)}, s32[256]{0:T(256)}, u32[]{:S(2)}) copy-start(s32[256]{0:T(256)} %param.17) | copy-start | bytes 3076
  27.6 215.1 %collective-permute-start.8 = (f32[16,1,256]{0,2,1:T(8,128)S(1)}, f32[16,1,256]{0,2,1:T(8,128)}, u32[]{:S(2)}, u32[]{:S(2)}) collective-permute-start(f32[16,1,256]{0,2,1:T(8,128)S(1)} %copy.253), channel_id=1, source_target_pairs={{0,1},{1,2},{2,3},{3,4},{4,5},{5,6},{6,7},{7,8},{8,9},{9,10},{10,1... | collective-permute-start | bytes 49160 | tf_op jit(solution)/shard_map/ppermute | solution.py:17
  201.9 7.9 %copy-start.5 = (f32[10,128,256]{1,0,2:T(8,128)S(1)}, f32[10,128,256]{1,0,2:T(8,128)}, u32[]{:S(2)}) copy-start(f32[10,128,256]{1,0,2:T(8,128)} %copy.222) | copy-start | bytes 3932164
  201.9 16.6 %collective-permute-start.3 = (f32[16,128,1]{1,0,2:T(8,128)}, f32[16,128,1]{1,0,2:T(8,128)S(1)}, u32[]{:S(2)}, u32[]{:S(2)}) collective-permute-start(f32[16,128,1]{1,0,2:T(8,128)} %copy.226), channel_id=1, source_target_pairs={{0,16},{16,32},{32,48},{48,64},{64,80},{80,96},{96,112},{112,128},... | collective-permute-start | bytes 24584 | tf_op jit(solution)/shard_map/ppermute | solution.py:17
  201.9 20.4 %collective-permute-start.4 = (f32[16,128,1]{1,0,2:T(8,128)}, f32[16,128,1]{1,0,2:T(8,128)S(1)}, u32[]{:S(2)}, u32[]{:S(2)}) collective-permute-start(f32[16,128,1]{1,0,2:T(8,128)} %copy.228), channel_id=1, source_target_pairs={{16,0},{32,16},{48,32},{64,48},{80,64},{96,80},{112,96},{128,112},... | collective-permute-start | bytes 24584 | tf_op jit(solution)/shard_map/ppermute | solution.py:18
  207.8 25.1 %collective-permute-start.7 = (f32[10,1,256]{0,2,1:T(8,128)}, f32[10,1,256]{0,2,1:T(8,128)}, u32[]{:S(2)}, u32[]{:S(2)}) collective-permute-start(f32[10,1,256]{0,2,1:T(8,128)} %copy.252), channel_id=1, source_target_pairs={{1,0},{2,1},{3,2},{4,3},{5,4},{6,5},{7,6},{8,7},{9,8},{10,9},{11,1... | collective-permute-start | bytes 30728 | tf_op jit(solution)/shard_map/ppermute | solution.py:18
  218.5 20.5 %collective-permute-start.5 = (f32[8,1,256]{2,1,0:T(1,128)}, f32[8,1,256]{2,1,0:T(1,128)}, u32[]{:S(2)}, u32[]{:S(2)}) collective-permute-start(f32[8,1,256]{2,1,0:T(1,128)} %slice.211), channel_id=1, source_target_pairs={{0,1},{1,2},{2,3},{3,4},{4,5},{5,6},{6,7},{7,8},{8,9},{9,10},{10,1... | collective-permute-start | bytes 24584 | tf_op jit(solution)/shard_map/ppermute | solution.py:31
  222.2 19.4 %collective-permute-start.9 = (f32[16,1,256]{0,2,1:T(8,128)}, f32[16,1,256]{0,2,1:T(8,128)}, u32[]{:S(2)}, u32[]{:S(2)}) collective-permute-start(f32[16,1,256]{0,2,1:T(8,128)} %copy.254), channel_id=1, source_target_pairs={{1,0},{2,1},{3,2},{4,3},{5,4},{6,5},{7,6},{8,7},{9,8},{10,9},{11,1... | collective-permute-start | bytes 49160 | tf_op jit(solution)/shard_map/ppermute | solution.py:18
  227.8 5.1 %copy-start.12 = (f32[258,10]{1,0:T(8,128)S(1)}, f32[258,10]{1,0:T(8,128)}, u32[]{:S(2)}) copy-start(f32[258,10]{1,0:T(8,128)} %gather_fusion) | copy-start | bytes 30964
  227.8 5.1 %copy-start.16 = (pred[256]{0:T(512)(128)(4,1)S(1)}, pred[256]{0:T(512)(128)(4,1)}, u32[]{:S(2)}) copy-start(pred[256]{0:T(512)(128)(4,1)} %slice.255) | copy-start | bytes 772
  238.0 1.2 copy-start.10
  239.2 2.4 copy-start.11
  245.4 3.2 copy-start.2
  245.4 3.5 copy-start.4
  251.1 2.0 copy-start.1
  253.1 80.6 %copy-start.14 = (s32[1024]{0:T(1024)S(1)}, s32[1024]{0:T(1024)}, u32[]{:S(2)}) copy-start(s32[1024]{0:T(1024)} %pad_clamp_fusion) | copy-start | bytes 12292
  254.7 86.9 %collective-permute-start.10 = (f32[16,128,1]{1,0,2:T(8,128)S(1)}, f32[16,128,1]{1,0,2:T(8,128)}, u32[]{:S(2)}, u32[]{:S(2)}) collective-permute-start(f32[16,128,1]{1,0,2:T(8,128)S(1)} %copy.241), channel_id=1, source_target_pairs={{0,16},{16,32},{32,48},{48,64},{64,80},{80,96},{96,112},{112,128},... | collective-permute-start | bytes 24584 | tf_op jit(solution)/shard_map/ppermute | solution.py:17
  259.1 84.7 %collective-permute-start.11 = (f32[16,128,1]{1,0,2:T(8,128)}, f32[16,128,1]{1,0,2:T(8,128)}, u32[]{:S(2)}, u32[]{:S(2)}) collective-permute-start(f32[16,128,1]{1,0,2:T(8,128)} %copy.243), channel_id=1, source_target_pairs={{16,0},{32,16},{48,32},{64,48},{80,64},{96,80},{112,96},{128,112},... | collective-permute-start | bytes 24584 | tf_op jit(solution)/shard_map/ppermute | solution.py:18
  331.8 22.1 %collective-permute-start.12 = (f32[16,1,256]{0,2,1:T(8,128)S(1)}, f32[16,1,256]{0,2,1:T(8,128)}, u32[]{:S(2)}, u32[]{:S(2)}) collective-permute-start(f32[16,1,256]{0,2,1:T(8,128)S(1)} %copy.255), channel_id=1, source_target_pairs={{0,1},{1,2},{2,3},{3,4},{4,5},{5,6},{6,7},{7,8},{8,9},{9,10},{10,1... | collective-permute-start | bytes 49160 | tf_op jit(solution)/shard_map/ppermute | solution.py:17
  337.1 15.0 %collective-permute-start.13 = (f32[16,1,256]{0,2,1:T(8,128)}, f32[16,1,256]{0,2,1:T(8,128)S(1)}, u32[]{:S(2)}, u32[]{:S(2)}) collective-permute-start(f32[16,1,256]{0,2,1:T(8,128)} %copy.256), channel_id=1, source_target_pairs={{1,0},{2,1},{3,2},{4,3},{5,4},{6,5},{7,6},{8,7},{9,8},{10,9},{11,1... | collective-permute-start | bytes 49160 | tf_op jit(solution)/shard_map/ppermute | solution.py:18
  352.1 0.7 copy-start.13
  354.9 3.8 %copy-start.3 = (f32[2,8,128,257]{3,2,1,0:T(8,128)S(1)}, f32[2,8,128,257]{3,2,1,0:T(8,128)}, u32[]{:S(2)}) copy-start(f32[2,8,128,257]{3,2,1,0:T(8,128)} %multiply_subtract_fusion) | copy-start | bytes 6316036
  354.9 4.4 %copy-start.6 = (f32[2,8,128,256]{3,2,1,0:T(8,128)S(1)}, f32[2,8,128,256]{3,2,1,0:T(8,128)}, u32[]{:S(2)}) copy-start(f32[2,8,128,256]{3,2,1,0:T(8,128)} %get-tuple-element.7) | copy-start | bytes 6291460
  354.9 4.7 %copy-start.7 = (f32[8,128,256]{2,1,0:T(8,128)S(1)}, f32[8,128,256]{2,1,0:T(8,128)}, u32[]{:S(2)}) copy-start(f32[8,128,256]{2,1,0:T(8,128)} %convert_element_type.3) | copy-start | bytes 3145732
where the time goes:
time: 364 us; the launch traced here: 362 us
  blocking collectives  213 us (59%)
  local copies, waits for them, and re-layouts  66.7 us (18%)
  other arithmetic  43.7 us (12%)
  starting transfers between devices  36.8 us (10%)
    all_gather x3, blocking collectives, partner_window(): gathered = lax.all_gather(top_rows, 'lon', axis=2, tiled=True)  213 us
    ppermute x6, starting transfers between devices, extended(): after = lax.ppermute(leading, axis, down)  16 us
    ppermute x6, starting transfers between devices, extended(): before = lax.ppermute(last, axis, up)  13.2 us
    unnamed x42, local copies, waits for them, and re-layouts  11.5 us
    sub x2, other arithmetic, tendency(): trans_u * 0.5 * (trac_lon[..., :-1] + trac_lon[..., 1:])  11.4 us
    slice x8, local copies, waits for them, and re-layouts, extended(): last = lax.slice_in_dim(array, length - width, length, axis=dim)  10.8 us
    gather x3, local copies, waits for them, and re-layouts, partner_window(): return jnp.take(gathered, wanted, axis=2)  9.24 us
  transfers between devices with their start and end apart: 14, of which 0 were waited for; matrix products, arithmetic and copies ran while one was open for 22% of the time, Pallas kernels for 0%

commit v1 on v0

--- a/solution.py
+++ b/solution.py
@@ -71,7 +71,8 @@
     wanted = jnp.concatenate(
         [(fold_partner[:1] + 1) % total, fold_partner, (fold_partner[-1:] - 1 + total) % total]
     )
-    gathered = lax.all_gather(top_rows, "lon", axis=2, tiled=True)
+    repeated = jnp.stack([top_rows] * lax.axis_size("lon"))
+    gathered = jnp.concatenate(lax.all_to_all(repeated, "lon", 0, 0), axis=2)
     return jnp.take(gathered, wanted, axis=2)
 
 

time: 364 us -> 184 us (0.51)
  the two profiles are of different devices: /device:TPU:116 before, /device:TPU:8 now
where the time goes in v1:
time: 184 us; the launch traced here: 182 us
  local copies, waits for them, and re-layouts  72.1 us (39%)
  starting transfers between devices  66.1 us (36%)
  other arithmetic  41.5 us (23%)
    all_to_all x3, starting transfers between devices, partner_window(): gathered = jnp.concatenate(lax.all_to_all(repeated, 'lon', 0, 0), axis=2)  25.5 us
    ppermute x6, starting transfers between devices, extended(): after = lax.ppermute(leading, axis, down)  20.9 us
    ppermute x6, starting transfers between devices, extended(): before = lax.ppermute(last, axis, up)  17.4 us
    unnamed x42, local copies, waits for them, and re-layouts  12.4 us
    slice x8, local copies, waits for them, and re-layouts, extended(): last = lax.slice_in_dim(array, length - width, length, axis=dim)  12.2 us
    sub x2, other arithmetic, tendency(): trans_u * 0.5 * (trac_lon[..., :-1] + trac_lon[..., 1:])  11.4 us
    gather x3, local copies, waits for them, and re-layouts, partner_window(): return jnp.take(gathered, wanted, axis=2)  8.42 us
    concatenate x4, local copies, waits for them, and re-layouts, extended(): array = jnp.concatenate([before, array, after], axis=dim)  8.23 us
  transfers between devices with their start and end apart: 17, of which 1 were waited for; matrix products, arithmetic and copies ran while one was open for 48% of the time, Pallas kernels for 0%

profile of v1, /device:TPU:8, one launch (start us, length us, event | category | flops | bytes accessed | tf_op | source)
XLA Modules:
  0.0 182.0 jit_solution(13373167446872437205)
XLA Ops:
  0.0 1.0 mul.221
  1.0 2.7 %convert_multiply_fusion = (f32[8,128,256]{2,1,0:T(8,128)S(1)}, f32[8,128,256]{2,1,0:T(8,128)}) fusion(f32[8,128,256]{2,1,0:T(8,128)} %param.13, s32[8,128,256]{2,1,0:T(8,128)} %param.14, f32[128,256]{1,0:T(8,128)S(1)} %mul.221), kind=kLoop, calls=%fused_computation.76 | loop fusion | flops 786432 | bytes 4325376 | tf_op jit(solution)/shard_map/mul | solution.py:131
  3.7 1.2 pad_maximum_fusion.8
  4.9 3.0 %copy.205 = f32[10,128,256]{1,2,0:T(8,128)} copy(f32[10,128,256]{2,1,0:T(8,128)} %pad_maximum_fusion.8) | data formatting | bytes 2621440 | tf_op jit(solution)/shard_map/concatenate | solution.py:96
  7.9 0.8 fusion.28
  8.7 3.1 %collective-permute-start.1 = (f32[10,128,1]{1,2,0:T(1,128)S(1)}, f32[10,128,1]{1,2,0:T(1,128)S(1)}, u32[]{:S(2)}, u32[]{:S(2)}) collective-permute-start(f32[10,128,1]{1,2,0:T(1,128)S(1)} %get-tuple-element.27), channel_id=1, source_target_pairs={{0,16},{16,32},{32,48},{48,64},{64,80},{80,96},{96,112},{112,128},... | collective-permute-start | bytes 15368 | tf_op jit(solution)/shard_map/ppermute | solution.py:17
  11.8 5.4 %collective-permute-start.2 = (f32[10,128,1]{1,2,0:T(1,128)S(1)}, f32[10,128,1]{1,2,0:T(1,128)S(1)}, u32[]{:S(2)}, u32[]{:S(2)}) collective-permute-start(f32[10,128,1]{1,2,0:T(1,128)S(1)} %get-tuple-element.28), channel_id=1, source_target_pairs={{16,0},{32,16},{48,32},{64,48},{80,64},{96,80},{112,96},{128,112},... | collective-permute-start | bytes 15368 | tf_op jit(solution)/shard_map/ppermute | solution.py:18
  17.2 2.6 %copy.203 = f32[8,128,256]{1,0,2:T(8,128)} copy(f32[8,128,256]{2,1,0:T(8,128)} %param.11) | data formatting | bytes 2097152 | tf_op args[1]
  20.4 1.5 fusion.29
  22.0 1.9 %collective-permute-start.6 = (f32[10,1,256]{2,1,0:T(1,128)}, f32[10,1,256]{2,1,0:T(1,128)}, u32[]{:S(2)}, u32[]{:S(2)}) collective-permute-start(f32[10,1,256]{2,1,0:T(1,128)} %get-tuple-element.31), channel_id=1, source_target_pairs={{0,1},{1,2},{2,3},{3,4},{4,5},{5,6},{6,7},{7,8},{8,9},{9,10},{10,1... | collective-permute-start | bytes 30728 | tf_op jit(solution)/shard_map/ppermute | solution.py:17
  24.6 0.7 stack.6
  25.3 8.8 %all-to-all-start = ((f32[16,10,1,256]{3,2,1,0:T(1,128)}), f32[16,10,1,256]{3,2,1,0:T(1,128)}, u32[]{:S(2)}, u32[]{:S(2)}) async-start(f32[16,10,1,256]{3,2,1,0:T(1,128)} %stack.6), calls=%async_computation | async-start | bytes 327680 | tf_op jit(solution)/shard_map/all_to_all | solution.py:75
  34.8 4.0 %collective-permute-start.8 = (f32[16,1,256]{2,1,0:T(1,128)}, f32[16,1,256]{2,1,0:T(1,128)}, u32[]{:S(2)}, u32[]{:S(2)}) collective-permute-start(f32[16,1,256]{2,1,0:T(1,128)} %get-tuple-element.22), channel_id=1, source_target_pairs={{0,1},{1,2},{2,3},{3,4},{4,5},{5,6},{6,7},{7,8},{8,9},{9,10},{10,1... | collective-permute-start | bytes 49160 | tf_op jit(solution)/shard_map/ppermute | solution.py:17
  38.7 1.7 fusion.26
  42.4 1.5 constant_dynamic-update-slice_fusion
  45.3 2.9 %copy.209 = f32[10,128,256]{1,0,2:T(8,128)} copy(f32[10,128,256]{2,1,0:T(8,128)} %pad_maximum_fusion.8) | data formatting | bytes 2621440 | tf_op jit(solution)/shard_map/concatenate | solution.py:96
  48.9 2.1 %copy.213 = f32[16,128,1]{1,0,2:T(8,128)} copy(f32[16,128,1]{2,1,0:T(8,128)} %get-tuple-element.20) | data formatting | bytes 16384 | tf_op jit(solution)/shard_map/slice | solution.py:15
  51.0 2.1 %copy.215 = f32[16,128,1]{1,0,2:T(8,128)} copy(f32[16,128,1]{2,1,0:T(8,128)} %get-tuple-element.21) | data formatting | bytes 16384 | tf_op jit(solution)/shard_map/slice | solution.py:16
  53.8 0.8 copy.238
  54.6 1.4 slice.217
  56.0 0.7 copy.239
  56.8 3.1 %collective-permute-start.3 = (f32[16,128,1]{1,0,2:T(8,128)}, f32[16,128,1]{1,0,2:T(8,128)}, u32[]{:S(2)}, u32[]{:S(2)}) collective-permute-start(f32[16,128,1]{1,0,2:T(8,128)} %copy.213), channel_id=1, source_target_pairs={{0,16},{16,32},{32,48},{48,64},{64,80},{80,96},{96,112},{112,128},... | collective-permute-start | bytes 24584 | tf_op jit(solution)/shard_map/ppermute | solution.py:17
  59.9 2.5 %collective-permute-start.4 = (f32[16,128,1]{1,0,2:T(8,128)}, f32[16,128,1]{1,0,2:T(8,128)}, u32[]{:S(2)}, u32[]{:S(2)}) collective-permute-start(f32[16,128,1]{1,0,2:T(8,128)} %copy.215), channel_id=1, source_target_pairs={{16,0},{32,16},{48,32},{64,48},{80,64},{96,80},{112,96},{128,112},... | collective-permute-start | bytes 24584 | tf_op jit(solution)/shard_map/ppermute | solution.py:18
  62.4 1.0 maximum_bitcast_fusion
  63.5 2.1 %collective-permute-start.7 = (f32[10,1,256]{0,2,1:T(8,128)}, f32[10,1,256]{0,2,1:T(8,128)S(1)}, u32[]{:S(2)}, u32[]{:S(2)}) collective-permute-start(f32[10,1,256]{0,2,1:T(8,128)} %copy.238), channel_id=1, source_target_pairs={{1,0},{2,1},{3,2},{4,3},{5,4},{6,5},{7,6},{8,7},{9,8},{10,9},{11,1... | collective-permute-start | bytes 30728 | tf_op jit(solution)/shard_map/ppermute | solution.py:18
  65.6 2.9 %fusion.14 = (f32[8,128,257]{1,0,2:T(8,128)}, f32[8,128,257]{1,0,2:T(8,128)}) fusion(f32[8,128,256]{1,0,2:T(8,128)} %copy.203, f32[8,128,1]{1,0,2:T(8,128)} %collective-permute-done, f32[128,257]{0,1:T(8,128)S(1)} %get-tuple-element.35, f32[10,128,1]{1,0,2:T(8,128)S(1)} %copy.211, f32[10,128,256]{1,0,2:T(8,128)S(1)} %copy-done.5, ...), kind=kLoop, calls=%fused_computation.42 | loop fusion | flops 2368512 | bytes 4873728 | tf_op jit(solution)/shard_map/mul | solution.py:52
  68.5 2.9 %copy.212 = f32[8,128,257]{2,1,0:T(8,128)} copy(f32[8,128,257]{1,0,2:T(8,128)} %get-tuple-element.14) | data formatting | bytes 2105344 | tf_op jit(solution)/shard_map/mul | solution.py:52
  71.4 2.8 %copy.217 = f32[8,128,257]{2,1,0:T(8,128)} copy(f32[8,128,257]{1,0,2:T(8,128)} %get-tuple-element.15) | data formatting | bytes 2105344 | tf_op jit(solution)/shard_map/div | solution.py:51
  74.2 2.3 %collective-permute-start.5 = (f32[8,1,256]{2,1,0:T(1,128)}, f32[8,1,256]{2,1,0:T(1,128)}, u32[]{:S(2)}, u32[]{:S(2)}) collective-permute-start(f32[8,1,256]{2,1,0:T(1,128)} %slice.217), channel_id=1, source_target_pairs={{0,1},{1,2},{2,3},{3,4},{4,5},{5,6},{6,7},{7,8},{8,9},{9,10},{10,1... | collective-permute-start | bytes 24584 | tf_op jit(solution)/shard_map/ppermute | solution.py:31
  76.5 2.0 %copy.214 = f32[2,8,128,1]{3,2,1,0:T(8,128)} copy(f32[2,8,128,1]{2,1,0,3:T(8,128)} %bitcast.4) | data formatting | bytes 16384 | tf_op jit(solution)/shard_map/concatenate | solution.py:19
  78.5 4.2 %collective-permute-start.9 = (f32[16,1,256]{0,2,1:T(8,128)}, f32[16,1,256]{0,2,1:T(8,128)}, u32[]{:S(2)}, u32[]{:S(2)}) collective-permute-start(f32[16,1,256]{0,2,1:T(8,128)} %copy.239), channel_id=1, source_target_pairs={{1,0},{2,1},{3,2},{4,3},{5,4},{6,5},{7,6},{8,7},{9,8},{10,9},{11,1... | collective-permute-start | bytes 49160 | tf_op jit(solution)/shard_map/ppermute | solution.py:18
  82.7 2.0 %copy.216 = f32[2,8,128,1]{3,2,1,0:T(8,128)} copy(f32[2,8,128,1]{2,1,0,3:T(8,128)} %bitcast.5) | data formatting | bytes 16384 | tf_op jit(solution)/shard_map/concatenate | solution.py:19
  84.8 5.1 %multiply_subtract_fusion.1 = f32[2,8,128,257]{3,2,1,0:T(8,128)} fusion(f32[2,8,128,1]{3,2,1,0:T(8,128)} %copy.216, f32[2,8,128,256]{3,2,1,0:T(8,128)S(1)} %copy-done, f32[2,8,128,1]{3,2,1,0:T(8,128)} %copy.214, f32[8,128,257]{2,1,0:T(8,128)} %copy.217, f32[8,128,257]{2,1,0:T(8,128)} %copy.212), kind=kLoop, calls=%fused_computation.8 | loop fusion | flops 3684352 | bytes 6324224 | tf_op jit(solution)/shard_map/sub | solution.py:52
  90.6 7.7 %all-to-all-start.1 = ((f32[16,16,1,256]{3,1,2,0:T(8,128)}), f32[16,16,1,256]{3,1,2,0:T(8,128)}, u32[]{:S(2)}, u32[]{:S(2)}) async-start(f32[16,16,1,256]{3,1,2,0:T(8,128)} %stack.7), calls=%async_computation.1 | async-start | bytes 524288 | tf_op jit(solution)/shard_map/all_to_all | solution.py:75
  98.3 2.6 %copy.218 = f32[10,1,16,256]{0,3,2,1:T(8,128)} copy(f32[10,1,16,256]{3,1,0,2:T(1,128)} %bitcast.7) | data formatting | bytes 327680 | tf_op jit(solution)/shard_map/reshape | solution.py:75
  100.9 3.2 %gather_fusion = f32[258,10]{1,0:T(8,128)} fusion(f32[10,4096]{0,1:T(8,128)} %bitcast.57, s32[1024]{0:T(1024)S(1)} %copy-done.13), kind=kCustom, calls=%fused_computation.2 | custom fusion | bytes 21672 | tf_op jit(solution)/shard_map/jit(_take)/gather | solution.py:76
  104.7 1.1 fusion.21
  106.6 1.0 maximum_maximum_fusion
  107.8 2.4 %fusion.11 = (f32[8,129,256]{2,1,0:T(8,128)}, f32[8,129,256]{2,1,0:T(8,128)}) fusion(f32[8,128,256]{2,1,0:T(8,128)S(1)} %copy-done.10, f32[8,1,256]{2,1,0:T(1,128)} %collective-permute-done.5, f32[129,256]{1,0:T(8,128)S(1)} %get-tuple-element.8, f32[10,129,256]{2,1,0:T(8,128)S(1)} %get-tuple-element.30, f32[10,129,256]{2,1,0:T(8,128)S(1)} %get-tuple-element.29, ...), kind=kLoop, calls=%fused_computation.35 | loop fusion | flops 1849344 | bytes 5680128 | tf_op jit(solution)/shard_map/mul | solution.py:60
  110.8 2.9 %copy.222 = f32[16,1,16,256]{0,3,2,1:T(8,128)} copy(f32[16,1,16,256]{3,0,1,2:T(8,128)} %bitcast.16) | data formatting | bytes 524288 | tf_op jit(solution)/shard_map/reshape | solution.py:75
  113.7 2.6 %gather_fusion.1 = f32[258,16]{1,0:T(8,128)S(1)} fusion(f32[16,4096]{0,1:T(8,128)} %bitcast.59, s32[1024]{0:T(1024)S(1)} %copy-done.12), kind=kCustom, calls=%fused_computation.clone | custom fusion | bytes 34056 | tf_op jit(solution)/shard_map/jit(_take)/gather | solution.py:76
  116.3 1.0 fusion.20
  117.5 1.6 dynamic-update-slice.1
  119.1 2.9 %multiply_subtract_fusion.3 = f32[2,8,129,256]{3,2,1,0:T(8,128)S(1)} fusion(f32[2,8,129,256]{3,2,1,0:T(8,128)} %dynamic-update-slice.1, f32[2,8,128,256]{3,2,1,0:T(8,128)S(1)} %copy-done, f32[2,8,1,256]{3,2,1,0:T(1,128)} %bitcast.15, f32[8,129,256]{2,1,0:T(8,128)} %get-tuple-element.13, f32[8,129,256]{2,1,0:T(8,128)} %get-tuple-element.12), kind=kLoop, calls=%fused_computation.13 | loop fusion | flops 3170304 | bytes 8454144 | tf_op jit(solution)/shard_map/sub | solution.py:60
  122.6 2.2 %multiply_add_fusion = (f32[2,8,128,256]{3,2,1,0:T(8,128)S(1)}, f32[2,8,128,256]{3,2,1,0:T(8,128)}) fusion(f32[2,8,128,256]{3,2,1,0:T(8,128)S(1)} %copy-done, f32[8,128,256]{2,1,0:T(8,128)S(1)} %copy-done.4, f32[2,8,129,256]{3,2,1,0:T(8,128)S(1)} %multiply_subtract_fusion.3, f32[2,8,128,257]{3,2,1,0:T(8,128)S(1)} %copy-done.2), kind=kLoop, calls=%fused_computation.27 | loop fusion | flops 3670016 | bytes 15728640 | tf_op jit(solution)/shard_map/add | solution.py:121
  124.9 1.3 copy-done.1
  127.6 0.7 stack.8
  128.3 9.0 %all-to-all-start.2 = ((f32[16,16,1,256]{3,1,2,0:T(8,128)}), f32[16,16,1,256]{3,1,2,0:T(8,128)S(1)}, u32[]{:S(2)}, u32[]{:S(2)}) async-start(f32[16,16,1,256]{3,1,2,0:T(8,128)} %stack.8), calls=%async_computation.2 | async-start | bytes 524288 | tf_op jit(solution)/shard_map/all_to_all | solution.py:75
  137.3 3.2 %fusion.24 = (f32[16,128,1]{2,1,0:T(8,128)}, f32[16,128,1]{2,1,0:T(8,128)}) fusion(f32[16,128,256]{2,1,0:T(8,128)} %bitcast.56), kind=kLoop, calls=%fused_computation.77 | loop fusion | bytes 32768 | tf_op jit(solution)/shard_map/slice | solution.py:15
  140.5 1.6 copy.226
  142.1 3.5 %collective-permute-start.10 = (f32[16,128,1]{1,0,2:T(8,128)S(1)}, f32[16,128,1]{1,0,2:T(8,128)}, u32[]{:S(2)}, u32[]{:S(2)}) collective-permute-start(f32[16,128,1]{1,0,2:T(8,128)S(1)} %copy.226), channel_id=1, source_target_pairs={{0,16},{16,32},{32,48},{48,64},{64,80},{80,96},{96,112},{112,128},... | collective-permute-start | bytes 24584 | tf_op jit(solution)/shard_map/ppermute | solution.py:17
  145.6 2.1 %copy.228 = f32[16,128,1]{1,0,2:T(8,128)} copy(f32[16,128,1]{2,1,0:T(8,128)} %get-tuple-element.17) | data formatting | bytes 16384 | tf_op jit(solution)/shard_map/slice | solution.py:16
  147.7 2.2 %collective-permute-start.11 = (f32[16,128,1]{1,0,2:T(8,128)}, f32[16,128,1]{1,0,2:T(8,128)}, u32[]{:S(2)}, u32[]{:S(2)}) collective-permute-start(f32[16,128,1]{1,0,2:T(8,128)} %copy.228), channel_id=1, source_target_pairs={{16,0},{32,16},{48,32},{64,48},{80,64},{96,80},{112,96},{128,112},... | collective-permute-start | bytes 24584 | tf_op jit(solution)/shard_map/ppermute | solution.py:18
  149.9 2.3 %convert_element_type.3 = f32[8,128,256]{2,1,0:T(8,128)} convert(s32[8,128,256]{2,1,0:T(8,128)} %param.14) | non-fusion elementwise | flops 262144 | bytes 2097152 | tf_op jit(solution)/shard_map/convert_element_type | solution.py:130
  152.2 1.9 %collective-permute-start.12 = (f32[16,1,256]{2,1,0:T(1,128)}, f32[16,1,256]{2,1,0:T(1,128)}, u32[]{:S(2)}, u32[]{:S(2)}) collective-permute-start(f32[16,1,256]{2,1,0:T(1,128)} %get-tuple-element.18), channel_id=1, source_target_pairs={{0,1},{1,2},{2,3},{3,4},{4,5},{5,6},{6,7},{7,8},{8,9},{9,10},{10,1... | collective-permute-start | bytes 49160 | tf_op jit(solution)/shard_map/ppermute | solution.py:17
  154.1 0.8 copy.240
  154.9 4.5 %collective-permute-start.13 = (f32[16,1,256]{0,2,1:T(8,128)}, f32[16,1,256]{0,2,1:T(8,128)S(1)}, u32[]{:S(2)}, u32[]{:S(2)}) collective-permute-start(f32[16,1,256]{0,2,1:T(8,128)} %copy.240), channel_id=1, source_target_pairs={{1,0},{2,1},{3,2},{4,3},{5,4},{6,5},{7,6},{8,7},{9,8},{10,9},{11,1... | collective-permute-start | bytes 49160 | tf_op jit(solution)/shard_map/ppermute | solution.py:18
  159.4 2.1 %copy.227 = f32[2,8,128,1]{3,2,1,0:T(8,128)} copy(f32[2,8,128,1]{2,1,0,3:T(8,128)} %bitcast.25) | data formatting | bytes 16384 | tf_op jit(solution)/shard_map/concatenate | solution.py:19
  161.5 2.0 %copy.229 = f32[2,8,128,1]{3,2,1,0:T(8,128)} copy(f32[2,8,128,1]{2,1,0,3:T(8,128)} %bitcast.26) | data formatting | bytes 16384 | tf_op jit(solution)/shard_map/concatenate | solution.py:19
  163.6 6.3 %multiply_subtract_fusion = f32[2,8,128,257]{3,2,1,0:T(8,128)} fusion(f32[2,8,128,1]{3,2,1,0:T(8,128)} %copy.229, f32[2,8,128,256]{3,2,1,0:T(8,128)} %copy-done.1, f32[2,8,128,1]{3,2,1,0:T(8,128)} %copy.227, f32[8,128,257]{2,1,0:T(8,128)} %copy.217, f32[8,128,257]{2,1,0:T(8,128)} %copy.212), kind=kLoop, calls=%fused_computation.7 | loop fusion | flops 3684352 | bytes 6324224 | tf_op jit(solution)/shard_map/sub | solution.py:52
  169.9 1.9 %copy.231 = f32[16,1,16,256]{0,3,2,1:T(8,128)} copy(f32[16,1,16,256]{3,0,1,2:T(8,128)S(1)} %bitcast.66) | data formatting | bytes 524288 | tf_op jit(solution)/shard_map/reshape | solution.py:75
  171.8 2.6 %gather_fusion.2 = f32[258,16]{1,0:T(8,128)S(1)} fusion(f32[16,4096]{0,1:T(8,128)} %bitcast.58, s32[1024]{0:T(1024)S(1)} %copy-done.12), kind=kCustom, calls=%fused_computation.1.clone | custom fusion | bytes 34056 | tf_op jit(solution)/shard_map/jit(_take)/gather | solution.py:76
  174.7 3.5 %multiply_subtract_fusion.2 = f32[2,8,129,256]{3,2,1,0:T(8,128)S(1)} fusion(f32[2,8,1,256]{3,2,1,0:T(1,128)S(1)} %copy.234, f32[2,8,128,256]{3,2,1,0:T(8,128)} %copy-done.1, f32[2,8,1,256]{3,2,1,0:T(1,128)} %bitcast.27, f32[8,129,256]{2,1,0:T(8,128)} %get-tuple-element.13, f32[8,129,256]{2,1,0:T(8,128)} %get-tuple-element.12), kind=kLoop, calls=%fused_computation.12 | loop fusion | flops 3698688 | bytes 6356992 | tf_op jit(solution)/shard_map/sub | solution.py:60
  179.4 2.6 %fusion.9 = f32[2,8,128,256]{3,2,1,0:T(8,128)} fusion(f32[2,8,128,256]{3,2,1,0:T(8,128)S(1)} %copy-done, f32[2,8,128,256]{3,2,1,0:T(8,128)S(1)} %copy-done.6, f32[2,8,129,256]{3,2,1,0:T(8,128)S(1)} %multiply_subtract_fusion.2, f32[2,8,128,257]{3,2,1,0:T(8,128)S(1)} %copy-done.3, f32[8,128,256]{2,1,0:T(8,128)S(1)} %copy-done.4, f32[8,128,256]{2,1,0:T(8,128)S(1)} %copy-done.7), kind=kLoop, calls=%fused_computation.28 | loop fusion | flops 4718592 | bytes 16777216 | tf_op jit(solution)/shard_map/mul | solution.py:126
  (75 shorter events, 11.8 us)
Async XLA Ops:
  1.0 2.8 %copy-start.8 = (f32[128,256]{1,0:T(8,128)S(1)}, f32[128,256]{1,0:T(8,128)}, u32[]{:S(2)}) copy-start(f32[128,256]{1,0:T(8,128)} %param.15) | copy-start | bytes 393220
  1.0 2.7 %copy-start.9 = (f32[128,256]{1,0:T(8,128)S(1)}, f32[128,256]{1,0:T(8,128)}, u32[]{:S(2)}) copy-start(f32[128,256]{1,0:T(8,128)} %param.16) | copy-start | bytes 393220
  4.9 29.2 %copy-start = (f32[2,8,128,256]{3,2,1,0:T(8,128)S(1)}, f32[2,8,128,256]{3,2,1,0:T(8,128)}, u32[]{:S(2)}) copy-start(f32[2,8,128,256]{3,2,1,0:T(8,128)} %param.10) | copy-start | bytes 6291460
  8.7 48.1 %collective-permute-start.1 = (f32[10,128,1]{1,2,0:T(1,128)S(1)}, f32[10,128,1]{1,2,0:T(1,128)S(1)}, u32[]{:S(2)}, u32[]{:S(2)}) collective-permute-start(f32[10,128,1]{1,2,0:T(1,128)S(1)} %get-tuple-element.27), channel_id=1, source_target_pairs={{0,16},{16,32},{32,48},{48,64},{64,80},{80,96},{96,112},{112,128},... | collective-permute-start | bytes 15368 | tf_op jit(solution)/shard_map/ppermute | solution.py:17
  11.8 48.1 %collective-permute-start.2 = (f32[10,128,1]{1,2,0:T(1,128)S(1)}, f32[10,128,1]{1,2,0:T(1,128)S(1)}, u32[]{:S(2)}, u32[]{:S(2)}) collective-permute-start(f32[10,128,1]{1,2,0:T(1,128)S(1)} %get-tuple-element.28), channel_id=1, source_target_pairs={{16,0},{32,16},{48,32},{64,48},{80,64},{96,80},{112,96},{128,112},... | collective-permute-start | bytes 15368 | tf_op jit(solution)/shard_map/ppermute | solution.py:18
  20.4 43.1 %collective-permute-start = (f32[8,128,1]{1,0,2:T(8,128)S(1)}, f32[8,128,1]{1,0,2:T(8,128)}, u32[]{:S(2)}, u32[]{:S(2)}) collective-permute-start(f32[8,128,1]{1,0,2:T(8,128)S(1)} %slice.252), channel_id=1, source_target_pairs={{0,16},{16,32},{32,48},{48,64},{64,80},{80,96},{96,112},{112,128},... | collective-permute-start | bytes 12296 | tf_op jit(solution)/shard_map/ppermute | solution.py:25
  22.0 83.9 %collective-permute-start.6 = (f32[10,1,256]{2,1,0:T(1,128)}, f32[10,1,256]{2,1,0:T(1,128)}, u32[]{:S(2)}, u32[]{:S(2)}) collective-permute-start(f32[10,1,256]{2,1,0:T(1,128)} %get-tuple-element.31), channel_id=1, source_target_pairs={{0,1},{1,2},{2,3},{3,4},{4,5},{5,6},{6,7},{7,8},{8,9},{9,10},{10,1... | collective-permute-start | bytes 30728 | tf_op jit(solution)/shard_map/ppermute | solution.py:17
  25.3 64.5 %all-to-all-start = ((f32[16,10,1,256]{3,2,1,0:T(1,128)}), f32[16,10,1,256]{3,2,1,0:T(1,128)}, u32[]{:S(2)}, u32[]{:S(2)}) async-start(f32[16,10,1,256]{3,2,1,0:T(1,128)} %stack.6), calls=%async_computation | async-start | bytes 327680 | tf_op jit(solution)/shard_map/all_to_all | solution.py:75
  34.8 5.7 %copy-start.14 = (s32[256]{0:T(256)S(1)}, s32[256]{0:T(256)}, u32[]{:S(2)}) copy-start(s32[256]{0:T(256)} %param.17) | copy-start | bytes 3076
  34.8 84.3 %collective-permute-start.8 = (f32[16,1,256]{2,1,0:T(1,128)}, f32[16,1,256]{2,1,0:T(1,128)}, u32[]{:S(2)}, u32[]{:S(2)}) collective-permute-start(f32[16,1,256]{2,1,0:T(1,128)} %get-tuple-element.22), channel_id=1, source_target_pairs={{0,1},{1,2},{2,3},{3,4},{4,5},{5,6},{6,7},{7,8},{8,9},{9,10},{10,1... | collective-permute-start | bytes 49160 | tf_op jit(solution)/shard_map/ppermute | solution.py:17
  56.8 8.8 %copy-start.5 = (f32[10,128,256]{1,0,2:T(8,128)S(1)}, f32[10,128,256]{1,0,2:T(8,128)}, u32[]{:S(2)}) copy-start(f32[10,128,256]{1,0,2:T(8,128)} %copy.209) | copy-start | bytes 3932164
  56.8 17.5 %collective-permute-start.3 = (f32[16,128,1]{1,0,2:T(8,128)}, f32[16,128,1]{1,0,2:T(8,128)}, u32[]{:S(2)}, u32[]{:S(2)}) collective-permute-start(f32[16,128,1]{1,0,2:T(8,128)} %copy.213), channel_id=1, source_target_pairs={{0,16},{16,32},{32,48},{48,64},{64,80},{80,96},{96,112},{112,128},... | collective-permute-start | bytes 24584 | tf_op jit(solution)/shard_map/ppermute | solution.py:17
  59.9 18.7 %collective-permute-start.4 = (f32[16,128,1]{1,0,2:T(8,128)}, f32[16,128,1]{1,0,2:T(8,128)}, u32[]{:S(2)}, u32[]{:S(2)}) collective-permute-start(f32[16,128,1]{1,0,2:T(8,128)} %copy.215), channel_id=1, source_target_pairs={{16,0},{32,16},{48,32},{64,48},{80,64},{96,80},{112,96},{128,112},... | collective-permute-start | bytes 24584 | tf_op jit(solution)/shard_map/ppermute | solution.py:18
  63.5 40.5 %collective-permute-start.7 = (f32[10,1,256]{0,2,1:T(8,128)}, f32[10,1,256]{0,2,1:T(8,128)S(1)}, u32[]{:S(2)}, u32[]{:S(2)}) collective-permute-start(f32[10,1,256]{0,2,1:T(8,128)} %copy.238), channel_id=1, source_target_pairs={{1,0},{2,1},{3,2},{4,3},{5,4},{6,5},{7,6},{8,7},{9,8},{10,9},{11,1... | collective-permute-start | bytes 30728 | tf_op jit(solution)/shard_map/ppermute | solution.py:18
  74.2 33.4 %collective-permute-start.5 = (f32[8,1,256]{2,1,0:T(1,128)}, f32[8,1,256]{2,1,0:T(1,128)}, u32[]{:S(2)}, u32[]{:S(2)}) collective-permute-start(f32[8,1,256]{2,1,0:T(1,128)} %slice.217), channel_id=1, source_target_pairs={{0,1},{1,2},{2,3},{3,4},{4,5},{5,6},{6,7},{7,8},{8,9},{9,10},{10,1... | collective-permute-start | bytes 24584 | tf_op jit(solution)/shard_map/ppermute | solution.py:31
  78.5 37.8 %collective-permute-start.9 = (f32[16,1,256]{0,2,1:T(8,128)}, f32[16,1,256]{0,2,1:T(8,128)}, u32[]{:S(2)}, u32[]{:S(2)}) collective-permute-start(f32[16,1,256]{0,2,1:T(8,128)} %copy.239), channel_id=1, source_target_pairs={{1,0},{2,1},{3,2},{4,3},{5,4},{6,5},{7,6},{8,7},{9,8},{10,9},{11,1... | collective-permute-start | bytes 49160 | tf_op jit(solution)/shard_map/ppermute | solution.py:18
  90.6 10.3 %copy-start.13 = (s32[1024]{0:T(1024)S(1)}, s32[1024]{0:T(1024)}, u32[]{:S(2)}) copy-start(s32[1024]{0:T(1024)} %pad_clamp_fusion.1) | copy-start | bytes 12292
  90.6 14.1 %copy-start.15 = (pred[256]{0:T(512)(128)(4,1)S(1)}, pred[256]{0:T(512)(128)(4,1)}, u32[]{:S(2)}) copy-start(pred[256]{0:T(512)(128)(4,1)} %slice.264) | copy-start | bytes 772
  90.6 20.2 %all-to-all-start.1 = ((f32[16,16,1,256]{3,1,2,0:T(8,128)}), f32[16,16,1,256]{3,1,2,0:T(8,128)}, u32[]{:S(2)}, u32[]{:S(2)}) async-start(f32[16,16,1,256]{3,1,2,0:T(8,128)} %stack.7), calls=%async_computation.1 | async-start | bytes 524288 | tf_op jit(solution)/shard_map/all_to_all | solution.py:75
  104.0 0.7 copy-start.11
  106.6 1.2 copy-start.10
  110.2 3.4 %copy-start.12 = (s32[1024]{0:T(1024)S(1)}, s32[1024]{0:T(1024)}, u32[]{:S(2)}) copy-start(s32[1024]{0:T(1024)} %pad_clamp_fusion) | copy-start | bytes 12292
  119.1 3.2 %copy-start.2 = (f32[2,8,128,257]{3,2,1,0:T(8,128)S(1)}, f32[2,8,128,257]{3,2,1,0:T(8,128)}, u32[]{:S(2)}) copy-start(f32[2,8,128,257]{3,2,1,0:T(8,128)} %multiply_subtract_fusion.1) | copy-start | bytes 6316036
  119.1 3.5 %copy-start.4 = (f32[8,128,256]{2,1,0:T(8,128)S(1)}, f32[8,128,256]{2,1,0:T(8,128)}, u32[]{:S(2)}) copy-start(f32[8,128,256]{2,1,0:T(8,128)} %get-tuple-element.34) | copy-start | bytes 3145732
  124.9 1.3 copy-start.1
  128.3 41.6 %all-to-all-start.2 = ((f32[16,16,1,256]{3,1,2,0:T(8,128)}), f32[16,16,1,256]{3,1,2,0:T(8,128)S(1)}, u32[]{:S(2)}, u32[]{:S(2)}) async-start(f32[16,16,1,256]{3,1,2,0:T(8,128)} %stack.8), calls=%async_computation.2 | async-start | bytes 524288 | tf_op jit(solution)/shard_map/all_to_all | solution.py:75
  142.1 17.3 %collective-permute-start.10 = (f32[16,128,1]{1,0,2:T(8,128)S(1)}, f32[16,128,1]{1,0,2:T(8,128)}, u32[]{:S(2)}, u32[]{:S(2)}) collective-permute-start(f32[16,128,1]{1,0,2:T(8,128)S(1)} %copy.226), channel_id=1, source_target_pairs={{0,16},{16,32},{32,48},{48,64},{64,80},{80,96},{96,112},{112,128},... | collective-permute-start | bytes 24584 | tf_op jit(solution)/shard_map/ppermute | solution.py:17
  147.7 13.8 %collective-permute-start.11 = (f32[16,128,1]{1,0,2:T(8,128)}, f32[16,128,1]{1,0,2:T(8,128)}, u32[]{:S(2)}, u32[]{:S(2)}) collective-permute-start(f32[16,128,1]{1,0,2:T(8,128)} %copy.228), channel_id=1, source_target_pairs={{16,0},{32,16},{48,32},{64,48},{80,64},{96,80},{112,96},{128,112},... | collective-permute-start | bytes 24584 | tf_op jit(solution)/shard_map/ppermute | solution.py:18
  152.2 22.5 %collective-permute-start.12 = (f32[16,1,256]{2,1,0:T(1,128)}, f32[16,1,256]{2,1,0:T(1,128)}, u32[]{:S(2)}, u32[]{:S(2)}) collective-permute-start(f32[16,1,256]{2,1,0:T(1,128)} %get-tuple-element.18), channel_id=1, source_target_pairs={{0,1},{1,2},{2,3},{3,4},{4,5},{5,6},{6,7},{7,8},{8,9},{9,10},{10,1... | collective-permute-start | bytes 49160 | tf_op jit(solution)/shard_map/ppermute | solution.py:17
  154.9 19.6 %collective-permute-start.13 = (f32[16,1,256]{0,2,1:T(8,128)}, f32[16,1,256]{0,2,1:T(8,128)S(1)}, u32[]{:S(2)}, u32[]{:S(2)}) collective-permute-start(f32[16,1,256]{0,2,1:T(8,128)} %copy.240), channel_id=1, source_target_pairs={{1,0},{2,1},{3,2},{4,3},{5,4},{6,5},{7,6},{8,7},{9,8},{10,9},{11,1... | collective-permute-start | bytes 49160 | tf_op jit(solution)/shard_map/ppermute | solution.py:18
  169.9 4.6 %copy-start.16 = (pred[256]{0:T(512)(128)(4,1)S(1)}, pred[256]{0:T(512)(128)(4,1)}, u32[]{:S(2)}) copy-start(pred[256]{0:T(512)(128)(4,1)} %slice.264) | copy-start | bytes 772
  174.7 3.8 %copy-start.3 = (f32[2,8,128,257]{3,2,1,0:T(8,128)S(1)}, f32[2,8,128,257]{3,2,1,0:T(8,128)}, u32[]{:S(2)}) copy-start(f32[2,8,128,257]{3,2,1,0:T(8,128)} %multiply_subtract_fusion) | copy-start | bytes 6316036
  174.7 4.5 %copy-start.6 = (f32[2,8,128,256]{3,2,1,0:T(8,128)S(1)}, f32[2,8,128,256]{3,2,1,0:T(8,128)}, u32[]{:S(2)}) copy-start(f32[2,8,128,256]{3,2,1,0:T(8,128)} %get-tuple-element.7) | copy-start | bytes 6291460
  174.7 4.7 %copy-start.7 = (f32[8,128,256]{2,1,0:T(8,128)S(1)}, f32[8,128,256]{2,1,0:T(8,128)}, u32[]{:S(2)}) copy-start(f32[8,128,256]{2,1,0:T(8,128)} %convert_element_type.3) | copy-start | bytes 3145732
